TPU v7x, 128 devices: a whole 4x4x4 slice. The times are simulated.
128 devices in a mesh: section: 2 (over core), cin: 8 (over z_hi, y), cout: 8 (over z_lo, x).
Axes of the slice: x: 4, y: 4, z: 4 (z_hi: 2, z_lo: 2; z = z_hi * 2 + z_lo), core: 2. Of those that a mesh axis runs over, the one named last changes fastest.
Arguments:
- inner_features: bfloat16 [2, 784, 2560], P('section', None, ('cin', 'cout')), may hold values from 0 to 2
- block_input: bfloat16 [2, 784, 5120], P('section', None, ('cin', 'cout')), may hold values from -6 to 6
- first_kernel: bfloat16 [9, 2560, 2560], P(None, 'cin', 'cout'), may hold values from -0.0546875 to 0.0546875
- expand_weight: bfloat16 [2560, 5120], P('cout', 'cin'), may hold values from -0.15625 to 0.15625
- reduce_weight: bfloat16 [5120, 5120], P(('cin', 'section'), 'cout'), may hold values from -0.125 to 0.125
- stride_kernel: bfloat16 [9, 5120, 5120], P(None, 'cout', ('section', 'cin')), may hold values from -0.0390625 to 0.0390625
- output_grad: bfloat16 [2, 196, 5120], P(None, None, ('section', 'cin', 'cout')), may hold values from -6 to 6
Outputs:
- inner_gradient: float32 [2, 784, 2560], P('section', None, ('cin', 'cout'))
- input_gradient: bfloat16 [2, 784, 5120], P('section', None, ('cin', 'cout'))
- first_gradient: float32 [9, 2560, 2560], P(None, 'cin', 'cout')
- expand_gradient: float32 [2560, 5120], P('cout', 'cin')
- reduce_gradient: float32 [5120, 5120], P(('cin', 'section'), 'cout')
- stride_gradient: float32 [9, 5120, 5120], P(None, 'cout', ('section', 'cin'))
All inputs are finite; a program needn't handle non-finite values.
Results may differ from a plain program's by a relative error of at most 0.013.
Values may be sent and summed in bfloat16 or wider, within the bound.
A program may use at most 192 MiB of HBM per device.

v0:
```python
import jax
import jax.numpy as jnp
from jax import lax
from jax.sharding import PartitionSpec as P

SIDE = 28


def smooth_gate(values):
    return values * jax.nn.sigmoid(values)


def gate_slope(values):
    logistic = jax.nn.sigmoid(values)
    return logistic * (1.0 + values * (1.0 - logistic))


def flatten_rows(images):
    return images.reshape(images.shape[0] * images.shape[1], images.shape[2])


def project(images, matrix):
    product = jnp.dot(flatten_rows(images), matrix, preferred_element_type=jnp.float32)
    return product.reshape(images.shape[0], images.shape[1], matrix.shape[1])


def project_back(grads, matrix):
    product = lax.dot_general(
        flatten_rows(grads), matrix, (((1,), (1,)), ((), ())), preferred_element_type=jnp.float32
    )
    return product.reshape(grads.shape[0], grads.shape[1], matrix.shape[0])


def outer_rows(left, right):
    return lax.dot_general(
        flatten_rows(left),
        flatten_rows(right),
        (((0,), (0,)), ((), ())),
        preferred_element_type=jnp.float32,
    )


def padded_grid(images, side):
    grid = images.reshape(images.shape[0], side, side, images.shape[2])
    return jnp.pad(grid, ((0, 0), (1, 1), (1, 1), (0, 0)))


def conv_same(images, kernel, side):
    padded = padded_grid(images, side)
    total = jnp.zeros((images.shape[0] * side * side, kernel.shape[2]), jnp.float32)
    for row in range(3):
        for column in range(3):
            window = padded[:, row : row + side, column : column + side, :].reshape(
                -1, images.shape[2]
            )
            total = total + jnp.dot(
                window, kernel[3 * row + column], preferred_element_type=jnp.float32
            )
    return total.reshape(images.shape[0], side * side, kernel.shape[2])


def conv_same_back(grads, kernel, side):
    padded = padded_grid(grads, side)
    total = jnp.zeros((grads.shape[0] * side * side, kernel.shape[1]), jnp.float32)
    for row in range(3):
        for column in range(3):
            window = padded[:, 2 - row : 2 - row + side, 2 - column : 2 - column + side, :].reshape(
                -1, grads.shape[2]
            )
            total = total + lax.dot_general(
                window,
                kernel[3 * row + column],
                (((1,), (1,)), ((), ())),
                preferred_element_type=jnp.float32,
            )
    return total.reshape(grads.shape[0], side * side, kernel.shape[1])


def conv_same_weight(images, grads, side):
    padded = padded_grid(images, side)
    flat = flatten_rows(grads)
    terms = []
    for row in range(3):
        for column in range(3):
            window = padded[:, row : row + side, column : column + side, :].reshape(
                -1, images.shape[2]
            )
            terms.append(
                lax.dot_general(
                    window, flat, (((0,), (0,)), ((), ())), preferred_element_type=jnp.float32
                )
            )
    return jnp.stack(terms)


def conv_half_back(grads, kernel, side):
    half = side // 2
    count = grads.shape[0]
    flat = flatten_rows(grads)
    canvas = None
    for row in range(3):
        for column in range(3):
            term = lax.dot_general(
                flat,
                kernel[3 * row + column],
                (((1,), (1,)), ((), ())),
                preferred_element_type=jnp.float32,
            )
            term = term.reshape(count, half, half, kernel.shape[1])
            placed = lax.pad(
                term,
                jnp.zeros((), term.dtype),
                ((0, 0, 0), (row, 3 - row, 1), (column, 3 - column, 1), (0, 0, 0)),
            )
            canvas = placed if canvas is None else canvas + placed
    return canvas[:, 1 : side + 1, 1 : side + 1, :].reshape(count, side * side, kernel.shape[1])


def conv_half_weight(images, grads, side):
    padded = padded_grid(images, side)
    flat = flatten_rows(grads)
    terms = []
    for row in range(3):
        for column in range(3):
            window = padded[:, row : row + side : 2, column : column + side : 2, :].reshape(
                -1, images.shape[2]
            )
            terms.append(
                lax.dot_general(
                    window, flat, (((0,), (0,)), ((), ())), preferred_element_type=jnp.float32
                )
            )
    return jnp.stack(terms)


def gather_outer(shard):
    return lax.all_gather(shard, "cout", axis=2, tiled=True)


def gather_inner(shard):
    return lax.all_gather(shard, "cin", axis=2, tiled=True)


def sum_inner(partial_value):
    return lax.psum_scatter(partial_value, "cin", scatter_dimension=2, tiled=True)


def sum_outer(partial_value):
    return lax.psum_scatter(partial_value, "cout", scatter_dimension=2, tiled=True)


def shards(
    inner_features,
    block_input,
    first_kernel,
    expand_weight,
    reduce_weight,
    stride_kernel,
    output_grad,
):
    feature_block = gather_outer(inner_features)
    first_hidden = sum_inner(conv_same(feature_block, first_kernel, SIDE))
    first_act = smooth_gate(first_hidden).astype(jnp.bfloat16)
    first_block = gather_inner(first_act)
    expanded = sum_outer(project(first_block, expand_weight))
    joined_pre = block_input.astype(jnp.float32) + expanded
    joined = smooth_gate(joined_pre).astype(jnp.bfloat16)
    joined_wide = gather_outer(joined)
    joined_pair = lax.all_to_all(joined_wide, "section", split_axis=2, concat_axis=0, tiled=True)
    hidden_part = project(joined_pair, reduce_weight)
    cotangent_block = gather_outer(output_grad)
    back_part = conv_half_back(cotangent_block, stride_kernel, SIDE)
    hidden_whole = lax.psum(hidden_part, ("section", "cin"))
    second_act = smooth_gate(hidden_whole).astype(jnp.bfloat16)
    back_whole = lax.psum(back_part, ("section", "cin"))
    masked_second = (back_whole * gate_slope(hidden_whole)).astype(jnp.bfloat16)
    stride_gradient = conv_half_weight(second_act, cotangent_block, SIDE)
    reduce_gradient = outer_rows(joined_pair, masked_second)
    joined_back = project_back(masked_second, reduce_weight)
    joined_home = lax.all_to_all(joined_back, "section", split_axis=0, concat_axis=2, tiled=True)
    back_joined = sum_outer(joined_home)
    input_gradient = (back_joined * gate_slope(joined_pre)).astype(jnp.bfloat16)
    input_wide = gather_outer(input_gradient)
    expand_local = outer_rows(first_block, input_wide)
    back_first = sum_inner(project_back(input_wide, expand_weight))
    masked_first = (back_first * gate_slope(first_hidden)).astype(jnp.bfloat16)
    masked_block = gather_inner(masked_first)
    inner_gradient = sum_outer(conv_same_back(masked_block, first_kernel, SIDE))
    first_local = conv_same_weight(feature_block, masked_block, SIDE)
    first_gradient, expand_gradient = (
        lax.psum(first_local.astype(jnp.bfloat16), "section").astype(jnp.float32),
        lax.psum(expand_local.astype(jnp.bfloat16), "section").astype(jnp.float32),
    )
    return (
        inner_gradient,
        input_gradient,
        first_gradient,
        expand_gradient,
        reduce_gradient,
        stride_gradient,
    )


def solution(mesh):
    return jax.shard_map(
        shards,
        mesh=mesh,
        in_specs=(
            P("section", None, ("cin", "cout")),
            P("section", None, ("cin", "cout")),
            P(None, "cin", "cout"),
            P("cout", "cin"),
            P(("cin", "section"), "cout"),
            P(None, "cout", ("section", "cin")),
            P(None, None, ("section", "cin", "cout")),
        ),
        out_specs=(
            P("section", None, ("cin", "cout")),
            P("section", None, ("cin", "cout")),
            P(None, "cin", "cout"),
            P("cout", "cin"),
            P(("cin", "section"), "cout"),
            P(None, "cout", ("section", "cin")),
        ),
        check_vma=False,
    )
```

profile of v0, /device:TPU:0, one launch (start us, length us, event | category | flops | bytes accessed | tf_op | source)
XLA Modules:
  0.0 957.9 jit_solution(9622084547646178098)
XLA Ops:
  7.2 30.3 %all_gather.19 = bf16[1,784,320]{1,2,0:T(8,128)(2,1)S(1)} all-gather(bf16[1,784,40]{1,2,0:T(8,128)(2,1)} %param.7), channel_id=1, replica_groups=mesh['section'=2,'cin'=8,'cout'=8] {'cout'}, dimensions={2}, use_global_device_ids=true | all-gather | bytes 564480 | tf_op jit(solution)/shard_map/all_gather | solution.py:137
  38.1 2.9 pad_slice_fusion.8
  42.1 2.3 reshape.187
  68.5 28.8 %all_gather.18 = bf16[2,196,320]{1,2,0:T(8,128)(2,1)S(1)} all-gather(bf16[2,196,40]{1,2,0:T(8,128)(2,1)S(1)} %copy-done.55), channel_id=1, replica_groups=mesh['section'=2,'cin'=8,'cout'=8] {'cout'}, dimensions={2}, use_global_device_ids=true | all-gather | bytes 282240 | tf_op jit(solution)/shard_map/all_gather | solution.py:137
  98.0 2.5 fusion.54
  102.0 16.4 %pad.56 = f32[2,28,28,640]{3,2,1,0:T(8,128)} pad(f32[2,14,14,640]{3,2,1,0:T(8,128)} %fusion.54, f32[]{:T(128)} %constant.3.clone.1), padding=0_0_0x1_0_1x1_0_1x0_0_0 | pad | bytes 5017604 | tf_op jit(solution)/shard_map/slice | solution.py:116
  118.4 11.1 %pad.55 = f32[2,28,28,640]{3,2,1,0:T(8,128)} pad(f32[2,14,14,640]{3,2,1,0:T(8,128)S(1)} %fusion.56, f32[]{:T(128)} %constant.3.clone.1), padding=0_0_0x1_0_1x0_1_1x0_0_0 | pad | bytes 5017604 | tf_op jit(solution)/shard_map/slice | solution.py:116
  131.0 11.1 %pad.53 = f32[2,28,28,640]{3,2,1,0:T(8,128)} pad(f32[2,14,14,640]{3,2,1,0:T(8,128)S(1)} %fusion.60, f32[]{:T(128)} %constant.3.clone.1), padding=0_0_0x0_1_1x1_0_1x0_0_0 | pad | bytes 5017604 | tf_op jit(solution)/shard_map/slice | solution.py:116
  143.6 11.1 %pad.52 = f32[2,28,28,640]{3,2,1,0:T(8,128)} pad(f32[2,14,14,640]{3,2,1,0:T(8,128)S(1)} %fusion.62, f32[]{:T(128)} %constant.3.clone.1), padding=0_0_0x0_1_1x0_1_1x0_0_0 | pad | bytes 5017604 | tf_op jit(solution)/shard_map/slice | solution.py:116
  156.2 11.3 %pad.41 = f32[2,30,30,640]{3,2,1,0:T(8,128)} pad(f32[2,14,14,640]{3,2,1,0:T(8,128)S(1)} %fusion.66, f32[]{:T(128)} %constant.3.clone.1), padding=0_0_0x0_3_1x2_1_1x0_0_0 | pad | bytes 5611524 | tf_op jit(solution)/shard_map/pad | solution.py:110
  168.9 11.2 %pad.39 = f32[2,30,30,640]{3,2,1,0:T(8,128)} pad(f32[2,14,14,640]{3,2,1,0:T(8,128)S(1)} %fusion.70, f32[]{:T(128)} %constant.3.clone.1), padding=0_0_0x0_3_1x0_3_1x0_0_0 | pad | bytes 5611524 | tf_op jit(solution)/shard_map/pad | solution.py:110
  181.6 11.3 %pad.40 = f32[2,30,30,640]{3,2,1,0:T(8,128)} pad(f32[2,14,14,640]{3,2,1,0:T(8,128)S(1)} %fusion.68, f32[]{:T(128)} %constant.3.clone.1), padding=0_0_0x0_3_1x1_2_1x0_0_0 | pad | bytes 5611524 | tf_op jit(solution)/shard_map/pad | solution.py:110
  194.4 11.1 %pad.74 = f32[2,28,29,640]{3,2,1,0:T(8,128)} pad(f32[2,14,14,640]{3,2,1,0:T(8,128)S(1)} %fusion.64, f32[]{:T(128)} %constant.3.clone.1), padding=0_0_0x0_1_1x0_2_1x0_0_0 | pad | bytes 5160964
  207.0 11.2 %pad.73 = f32[2,28,29,640]{3,2,1,0:T(8,128)} pad(f32[2,14,14,640]{3,2,1,0:T(8,128)S(1)} %fusion.58, f32[]{:T(128)} %constant.3.clone.1), padding=0_0_0x1_0_1x0_2_1x0_0_0 | pad | bytes 5160964
  219.1 36.6 %all_gather.20 = bf16[1,784,320]{1,2,0:T(8,128)(2,1)S(1)} all-gather(bf16[1,784,40]{1,2,0:T(8,128)(2,1)S(1)} %multiply_convert_fusion.4), channel_id=1, replica_groups=mesh['section'=2,'cin'=8,'cout'=8] {'cin'}, dimensions={2}, use_global_device_ids=true | all-gather | bytes 564480 | tf_op jit(solution)/shard_map/all_gather | solution.py:141
  257.3 4.1 copy.97
  261.8 6.8 add_add_fusion
  268.6 11.1 %fusion.4 = f32[2,28,28,640]{3,2,1,0:T(8,128)S(1)} fusion(f32[2,28,28,640]{3,2,1,0:T(8,128)} %pad.56, f32[2,28,28,640]{3,2,1,0:T(8,128)} %pad.55, f32[2,28,28,640]{3,2,1,0:T(8,128)} %pad.53, f32[2,28,28,640]{3,2,1,0:T(8,128)} %pad.52, f32[2,30,30,640]{3,2,1,0:T(8,128)S(1)} %add_add_fusion, f32[2,28,29,640]{3,2,1,0:T(8,128)} %pad.74, f32[2,28,29,640]{3,2,1,0:T(8,128)} %pad.73), kind=kLoop, calls=%fused_computation.6 | loop fusion | flops 6021120 | bytes 32112640 | tf_op jit(solution)/shard_map/add | solution.py:115
  279.7 3.1 copy.94
  282.8 2.2 copy.95
  286.3 58.8 %all-reduce.24.cloned.1.call-done = f32[1,784,640]{1,0,2:T(1,128)} async-done(((f32[1,784,640]{1,0,2:T(1,128)}), f32[1,784,640]{1,0,2:T(1,128)}) %all-reduce.24.cloned.1.call-update) | async-done | bytes 2007056
  346.9 31.0 %all_gather.21 = bf16[1,784,640]{1,2,0:T(8,128)(2,1)S(1)} all-gather(bf16[1,784,80]{1,2,0:T(8,128)(2,1)S(1)} %multiply_convert_fusion.2), channel_id=1, replica_groups=mesh['section'=2,'cin'=8,'cout'=8] {'cout'}, dimensions={2}, use_global_device_ids=true | all-gather | bytes 1128960 | tf_op jit(solution)/shard_map/all_gather | solution.py:137
  380.2 9.0 reduce
  389.1 3.1 reshape.245
  392.2 4.7 all_to_all.33
  396.9 2.6 reshape.246
  401.3 3.3 fusion.74
  404.7 195.4 %all-reduce.28.cloned.1.call-done = (f32[2,784,640]{2,1,0:T(8,128)}, f32[2,784,640]{2,1,0:T(8,128)}) async-done(((f32[2,784,640]{2,1,0:T(8,128)}, f32[2,784,640]{2,1,0:T(8,128)}), (f32[2,784,640]{2,1,0:T(8,128)}, f32[2,784,640]{2,1,0:T(8,128)})) %all-reduce.28.cloned.1.call-update) | async-done | bytes 8028176 | tf_op jit(solution)/shard_map/psum | solution.py:175
  600.2 5.1 multiply_convert_fusion
  606.6 5.6 all_to_all.34
  612.2 3.7 copy.100
  616.0 83.4 %all-reduce.26.cloned.1.call-done = f32[1,784,640]{1,0,2:T(1,128)} async-done(((f32[1,784,640]{1,0,2:T(1,128)}), f32[1,784,640]{1,0,2:T(1,128)}) %all-reduce.26.cloned.1.call-update) | async-done | bytes 2007056
  700.6 30.6 %all_gather.22 = bf16[1,784,640]{1,2,0:T(8,128)(2,1)S(1)} all-gather(bf16[1,784,80]{1,2,0:T(8,128)(2,1)S(1)} %fusion.85), channel_id=1, replica_groups=mesh['section'=2,'cin'=8,'cout'=8] {'cout'}, dimensions={2}, use_global_device_ids=true | all-gather | bytes 1128960 | tf_op jit(solution)/shard_map/all_gather | solution.py:137
  734.5 2.2 copy.104
  736.7 3.6 reshape.211
  741.9 5.0 fusion.137
  749.9 2.5 fusion.19
  752.3 2.4 fusion.18
  756.3 45.9 %reduce-scatter.16.cloned.1.call-done = f32[1,784,40]{1,2,0:T(8,128)} async-done(((f32[1,784,320]{1,2,0:T(8,128)}), f32[1,784,40]{1,2,0:T(8,128)}) %reduce-scatter.16.cloned.1.call-update) | async-done | bytes 125456
  803.2 35.5 %all_gather.23 = bf16[1,784,320]{1,2,0:T(8,128)(2,1)S(1)} all-gather(bf16[1,784,40]{1,2,0:T(8,128)(2,1)S(1)} %multiply_convert_fusion.3), channel_id=1, replica_groups=mesh['section'=2,'cin'=8,'cout'=8] {'cin'}, dimensions={2}, use_global_device_ids=true | all-gather | bytes 564480 | tf_op jit(solution)/shard_map/all_gather | solution.py:141
  841.3 6.5 pad_slice_fusion.4
  850.0 2.6 fusion.86
  856.9 2.2 reshape.206
  867.7 2.6 fusion.23
  870.3 2.6 fusion.25
  904.3 2.3 all-reduce.30.cloned.1.call-done
  906.7 4.1 convert_element_type.43
  911.7 38.9 %reduce-scatter.18.cloned.1.call-done = f32[1,784,40]{1,2,0:T(8,128)} async-done(((f32[1,784,320]{1,2,0:T(8,128)}), f32[1,784,40]{1,2,0:T(8,128)}) %reduce-scatter.18.cloned.1.call-update) | async-done | bytes 125456
  (224 shorter events, 110.2 us)
Async XLA Ops:
  7.2 394.1 %copy-start = (bf16[320,640]{1,0:T(8,128)(2,1)S(1)}, bf16[320,640]{1,0:T(8,128)(2,1)}, u32[]{:S(2)}) copy-start(bf16[320,640]{1,0:T(8,128)(2,1)} %param.11) | copy-start | bytes 1228804
  7.2 211.0 %reduce-scatter.14.cloned.1.call-start = ((), (), s32[]{:S(2)}) async-start(), calls=%async_computation.7 | async-start | bytes 1290240
  42.1 6.6 copy-start.1
  48.7 1.7 copy-start.19
  48.7 2.3 copy-start.18
  62.6 2.0 copy-start.24
  66.8 1.6 copy-start.55
  68.4 276.6 %all-reduce.24.cloned.1.call-start = ((), (), s32[]{:S(2)}) async-start(), calls=%async_computation.5 | async-start | bytes 4587520
  206.9 49.6 %copy-start.48 = (bf16[320,640]{1,0:T(8,128)(2,1)S(1)}, bf16[320,640]{1,0:T(8,128)(2,1)}, u32[]{:S(2)}) copy-start(bf16[320,640]{1,0:T(8,128)(2,1)} %param.10) | copy-start | bytes 1228804
  261.5 338.7 %all-reduce.28.cloned.1.call-start = ((), (), s32[]{:S(2)}) async-start(), calls=%async_computation.10 | async-start | bytes 16056320 | tf_op jit(solution)/shard_map/psum | solution.py:175
  282.8 2.2 copy-start.56
  282.8 63.3 %copy-start.52 = (bf16[1,784,80]{1,2,0:T(8,128)(2,1)S(1)}, bf16[1,784,80]{1,2,0:T(8,128)(2,1)}, u32[]{:S(2)}) copy-start(bf16[1,784,80]{1,2,0:T(8,128)(2,1)} %param.8) | copy-start | bytes 376324
  404.7 294.7 %all-reduce.26.cloned.1.call-start = ((), (), s32[]{:S(2)}) async-start(), calls=%async_computation.6 | async-start | bytes 4587520
  605.3 1.3 copy-start.3
  615.9 84.6 %copy-start.15 = (f32[1,784,80]{1,0,2:T(1,128)S(1)}, f32[1,784,80]{1,0,2:T(1,128)}, u32[]{:S(2)}) copy-start(f32[1,784,80]{1,0,2:T(1,128)} %copy-done.14) | copy-start | bytes 752644
  615.9 116.3 %copy-start.49 = (bf16[320,640]{1,0:T(8,128)(2,1)S(1)}, bf16[320,640]{1,0:T(8,128)(2,1)}, u32[]{:S(2)}) copy-start(bf16[320,640]{1,0:T(8,128)(2,1)} %param.10) | copy-start | bytes 1228804
  615.9 186.3 %reduce-scatter.16.cloned.1.call-start = ((), (), s32[]{:S(2)}) async-start(), calls=%async_computation.8 | async-start | bytes 1290240
  700.6 33.3 %copy-start.51 = (bf16[1,784,80]{1,2,0:T(8,128)(2,1)}, bf16[1,784,80]{1,2,0:T(8,128)(2,1)S(1)}, u32[]{:S(2)}) copy-start(bf16[1,784,80]{1,2,0:T(8,128)(2,1)S(1)} %fusion.85) | copy-start | bytes 376324
  732.2 2.0 copy-start.13
  733.9 172.8 %all-reduce.30.cloned.1.call-start = ((), (), s32[]{:S(2)}) async-start(), calls=%async_computation.11 | async-start | bytes 5242880 | tf_op jit(solution)/shard_map/psum | solution.py:191
  736.7 3.6 copy-start.5
  748.9 5.8 copy-start.10
  749.9 4.9 copy-start.36
  752.3 49.9 %copy-start.53 = (f32[1,784,40]{1,2,0:T(8,128)S(1)}, f32[1,784,40]{1,2,0:T(8,128)}, u32[]{:S(2)}) copy-start(f32[1,784,40]{1,2,0:T(8,128)} %reduce-scatter.14.cloned.1.call-done) | copy-start | bytes 376324
  754.8 84.3 %copy-start.27 = (bf16[784,320]{1,0:T(8,128)(2,1)S(1)}, bf16[784,320]{1,0:T(8,128)(2,1)}, u32[]{:S(2)}) copy-start(bf16[784,320]{1,0:T(8,128)(2,1)} %reshape.186) | copy-start | bytes 1505284
  838.7 1.6 copy-start.6
  841.3 8.6 copy-start.2
  867.7 5.2 copy-start.7
  867.7 5.2 copy-start.17
  870.3 5.0 copy-start.26
  872.9 3.7 copy-start.25
  874.1 3.7 copy-start.21
  875.3 3.8 copy-start.23
  879.1 1.6 copy-start.30
  880.4 70.2 %reduce-scatter.18.cloned.1.call-start = ((), (), s32[]{:S(2)}) async-start(), calls=%async_computation.9 | async-start | bytes 1290240
  880.8 1.6 copy-start.32
  885.2 1.4 copy-start.11
  886.6 1.6 copy-start.43
  888.2 1.4 copy-start.42
  888.2 1.6 copy-start.41
  889.8 2.0 copy-start.39
  892.2 3.4 copy-start.44
  893.2 3.7 copy-start.45
  895.6 4.1 copy-start.46
  896.9 4.1 copy-start.47
  898.3 4.1 copy-start.4
  898.3 4.1 copy-start.50
  906.7 4.1 copy-start.54
  (16 other events, 16.8 us)
Sparse Core Ops, SparseCore 0:
  68.6 69.3 reduce-scatter.13
  261.6 83.4 all-reduce.23
  404.8 195.3 all-reduce.27
  616.1 83.3 all-reduce.25
  734.0 68.1 reduce-scatter.15
  880.6 26.0 all-reduce.29
  909.6 40.9 reduce-scatter.17
where the time goes:
time: 967 us; the launch traced here: 958 us
  waiting for transfers between devices  425 us (44%)
  local copies, waits for them, and re-layouts  203 us (21%)
  blocking collectives  203 us (21%)
  matrix products  70.4 us (7%)
  other arithmetic  39.2 us (4%)
  between operations  15.9 us (2%)
    unnamed x12, waiting for transfers between devices  227 us
    psum x1, waiting for transfers between devices, shards(): back_whole = lax.psum(back_part, ('section', 'cin'))  195 us
    all_gather x4, blocking collectives, gather_outer(): return lax.all_gather(shard, 'cout', axis=2, tiled=True)  121 us
    all_gather x2, blocking collectives, gather_inner(): return lax.all_gather(shard, 'cin', axis=2, tiled=True)  72.1 us
    slice x5, local copies, waits for them, and re-layouts, conv_half_back(): canvas[:, 1:side + 1, 1:side + 1, :]  52.9 us
    unnamed x123, local copies, waits for them, and re-layouts  39.9 us
    pad x3, local copies, waits for them, and re-layouts, conv_half_back(): lax.pad(term, jnp.zeros((), term.dtype), ((0, 0, 0), (row, 3 - row, 1), (...  33.8 us
  transfers between devices with their start and end apart: 7, of which 6 were waited for; matrix products, arithmetic and copies ran while one was open for 20% of the time, Pallas kernels for 0%

commit v1 on v0

--- a/solution.py
+++ b/solution.py
@@ -172,7 +172,7 @@
     back_part = conv_half_back(cotangent_block, stride_kernel, SIDE)
     hidden_whole = lax.psum(hidden_part, ("section", "cin"))
     second_act = smooth_gate(hidden_whole).astype(jnp.bfloat16)
-    back_whole = lax.psum(back_part, ("section", "cin"))
+    back_whole = lax.psum(lax.psum(back_part, "section"), "cin")
     masked_second = (back_whole * gate_slope(hidden_whole)).astype(jnp.bfloat16)
     stride_gradient = conv_half_weight(second_act, cotangent_block, SIDE)
     reduce_gradient = outer_rows(joined_pair, masked_second)

time: 967 us -> 1060 us (1.096)
  waiting for transfers between devices: 425 us -> 473 us
  local copies, waits for them, and re-layouts: 203 us -> 235 us
    unnamed x12 -> x14, waiting for transfers between devices: 227 us -> 251 us
    psum x1 -> x3, waiting for transfers between devices: 195 us -> 219 us  [the longest x1 169 us: shards(): hidden_whole = lax.psum(hidden_part, ('section', 'cin'))]
    slice x5, local copies, waits for them, and re-layouts: 52.9 us -> 68.5 us  [conv_half_back(): canvas[:, 1:side + 1, 1:side + 1, :]]
    unnamed x123 -> x115, local copies, waits for them, and re-layouts: 39.9 us -> 51.7 us
  transfers between devices with their start and end apart: 7 -> 9, of which waited for: 6 -> 7; matrix products, arithmetic and copies ran while one was open for 20% -> 25% of each run, Pallas kernels for 0% -> 0%
where the time goes in v1:
time: 1060 us; the launch traced here: 1040 us
  waiting for transfers between devices  473 us (45%)
  local copies, waits for them, and re-layouts  235 us (22%)
  blocking collectives  208 us (20%)
  matrix products  71.1 us (7%)
  other arithmetic  38.7 us (4%)
  between operations  17.4 us (2%)
    unnamed x14, waiting for transfers between devices  251 us
    psum x1, waiting for transfers between devices, shards(): hidden_whole = lax.psum(hidden_part, ('section', 'cin'))  169 us
    all_gather x4, blocking collectives, gather_outer(): return lax.all_gather(shard, 'cout', axis=2, tiled=True)  126 us
    all_gather x2, blocking collectives, gather_inner(): return lax.all_gather(shard, 'cin', axis=2, tiled=True)  72.5 us
    slice x5, local copies, waits for them, and re-layouts, conv_half_back(): canvas[:, 1:side + 1, 1:side + 1, :]  68.5 us
    unnamed x115, local copies, waits for them, and re-layouts  51.7 us
    psum x2, waiting for transfers between devices, shards(): back_whole = lax.psum(lax.psum(back_part, 'section'), 'cin')  49.9 us
    pad x3, local copies, waits for them, and re-layouts, conv_half_back(): lax.pad(term, jnp.zeros((), term.dtype), ((0, 0, 0), (row, 3 - row, 1), (...  44.3 us
  transfers between devices with their start and end apart: 9, of which 7 were waited for; matrix products, arithmetic and copies ran while one was open for 25% of the time, Pallas kernels for 0%

profile of v1, /device:TPU:0, one launch (start us, length us, event | category | flops | bytes accessed | tf_op | source)
XLA Modules:
  0.0 1044.1 jit_solution(6055432681002926701)
XLA Ops:
  8.1 30.3 %all_gather.19 = bf16[1,784,320]{1,2,0:T(8,128)(2,1)S(1)} all-gather(bf16[1,784,40]{1,2,0:T(8,128)(2,1)} %param.7), channel_id=1, replica_groups=mesh['section'=2,'cin'=8,'cout'=8] {'cout'}, dimensions={2}, use_global_device_ids=true | all-gather | bytes 564480 | tf_op jit(solution)/shard_map/all_gather | solution.py:137
  39.7 6.2 pad_slice_fusion.8
  53.5 2.3 reshape.192
  69.8 28.8 %all_gather.18 = bf16[2,196,320]{1,2,0:T(8,128)(2,1)S(1)} all-gather(bf16[2,196,40]{1,2,0:T(8,128)(2,1)S(1)} %copy-done.49), channel_id=1, replica_groups=mesh['section'=2,'cin'=8,'cout'=8] {'cout'}, dimensions={2}, use_global_device_ids=true | all-gather | bytes 282240 | tf_op jit(solution)/shard_map/all_gather | solution.py:137
  101.0 2.5 fusion.66
  114.1 16.4 %pad.56 = f32[2,28,28,640]{3,2,1,0:T(8,128)} pad(f32[2,14,14,640]{3,2,1,0:T(8,128)} %fusion.54, f32[]{:T(128)} %constant.3.clone.1), padding=0_0_0x1_0_1x1_0_1x0_0_0 | pad | bytes 5017604 | tf_op jit(solution)/shard_map/slice | solution.py:116
  130.5 16.3 %pad.55 = f32[2,28,28,640]{3,2,1,0:T(8,128)} pad(f32[2,14,14,640]{3,2,1,0:T(8,128)} %fusion.56, f32[]{:T(128)} %constant.3.clone.1), padding=0_0_0x1_0_1x0_1_1x0_0_0 | pad | bytes 5017604 | tf_op jit(solution)/shard_map/slice | solution.py:116
  146.8 16.3 %pad.73 = f32[2,28,29,640]{3,2,1,0:T(8,128)} pad(f32[2,14,14,640]{3,2,1,0:T(8,128)} %fusion.58, f32[]{:T(128)} %constant.3.clone.1), padding=0_0_0x1_0_1x0_2_1x0_0_0 | pad | bytes 5160964
  163.2 16.3 %pad.53 = f32[2,28,28,640]{3,2,1,0:T(8,128)} pad(f32[2,14,14,640]{3,2,1,0:T(8,128)} %fusion.60, f32[]{:T(128)} %constant.3.clone.1), padding=0_0_0x0_1_1x1_0_1x0_0_0 | pad | bytes 5017604 | tf_op jit(solution)/shard_map/slice | solution.py:116
  179.5 16.3 %pad.52 = f32[2,28,28,640]{3,2,1,0:T(8,128)} pad(f32[2,14,14,640]{3,2,1,0:T(8,128)} %fusion.62, f32[]{:T(128)} %constant.3.clone.1), padding=0_0_0x0_1_1x0_1_1x0_0_0 | pad | bytes 5017604 | tf_op jit(solution)/shard_map/slice | solution.py:116
  195.8 16.4 %pad.74 = f32[2,28,29,640]{3,2,1,0:T(8,128)} pad(f32[2,14,14,640]{3,2,1,0:T(8,128)} %fusion.64, f32[]{:T(128)} %constant.3.clone.1), padding=0_0_0x0_1_1x0_2_1x0_0_0 | pad | bytes 5160964
  212.2 16.5 %pad.39 = f32[2,30,30,640]{3,2,1,0:T(8,128)} pad(f32[2,14,14,640]{3,2,1,0:T(8,128)} %fusion.70, f32[]{:T(128)} %constant.3.clone.1), padding=0_0_0x0_3_1x0_3_1x0_0_0 | pad | bytes 5611524 | tf_op jit(solution)/shard_map/pad | solution.py:110
  228.7 16.5 %pad.41 = f32[2,30,30,640]{3,2,1,0:T(8,128)} pad(f32[2,14,14,640]{3,2,1,0:T(8,128)} %fusion.66, f32[]{:T(128)} %constant.3.clone.1), padding=0_0_0x0_3_1x2_1_1x0_0_0 | pad | bytes 5611524 | tf_op jit(solution)/shard_map/pad | solution.py:110
  245.2 11.3 %pad.40 = f32[2,30,30,640]{3,2,1,0:T(8,128)} pad(f32[2,14,14,640]{3,2,1,0:T(8,128)S(1)} %fusion.68, f32[]{:T(128)} %constant.3.clone.1), padding=0_0_0x0_3_1x1_2_1x0_0_0 | pad | bytes 5611524 | tf_op jit(solution)/shard_map/pad | solution.py:110
  256.4 6.9 add_add_fusion
  263.4 9.5 fusion.4
  272.9 3.1 copy.94
  279.3 37.0 %all_gather.20 = bf16[1,784,320]{1,2,0:T(8,128)(2,1)S(1)} all-gather(bf16[1,784,40]{1,2,0:T(8,128)(2,1)S(1)} %multiply_convert_fusion.4), channel_id=1, replica_groups=mesh['section'=2,'cin'=8,'cout'=8] {'cin'}, dimensions={2}, use_global_device_ids=true | all-gather | bytes 564480 | tf_op jit(solution)/shard_map/all_gather | solution.py:141
  319.0 3.8 copy.97
  324.7 81.8 %all-reduce.31.cloned.1.call-done = f32[1,784,640]{1,0,2:T(1,128)} async-done(((f32[1,784,640]{1,0,2:T(1,128)}), f32[1,784,640]{1,0,2:T(1,128)}) %all-reduce.31.cloned.1.call-update) | async-done | bytes 2007056
  408.3 35.8 %all_gather.21 = bf16[1,784,640]{1,2,0:T(8,128)(2,1)S(1)} all-gather(bf16[1,784,80]{1,2,0:T(8,128)(2,1)S(1)} %multiply_convert_fusion.2), channel_id=1, replica_groups=mesh['section'=2,'cin'=8,'cout'=8] {'cout'}, dimensions={2}, use_global_device_ids=true | all-gather | bytes 1128960 | tf_op jit(solution)/shard_map/all_gather | solution.py:137
  446.4 9.0 reduce
  455.3 3.1 reshape.245
  458.4 4.7 all_to_all.33
  463.1 2.6 reshape.246
  467.5 3.3 fusion.74
  471.0 49.8 %all-reduce.27.cloned.1.call-done = f32[2,784,640]{2,1,0:T(8,128)} async-done(((f32[2,784,640]{2,1,0:T(8,128)}), f32[2,784,640]{2,1,0:T(8,128)}) %all-reduce.27.cloned.1.call-update) | async-done | bytes 4014096 | tf_op jit(solution)/shard_map/psum | solution.py:175
  520.8 168.9 %all-reduce.29.cloned.1.call-done = f32[2,784,640]{2,1,0:T(8,128)} async-done(((f32[2,784,640]{2,1,0:T(8,128)}), f32[2,784,640]{2,1,0:T(8,128)}) %all-reduce.29.cloned.1.call-update) | async-done | bytes 4014096 | tf_op jit(solution)/shard_map/psum | solution.py:173
  689.7 5.1 multiply_convert_fusion
  696.2 5.6 all_to_all.34
  701.7 3.7 copy.100
  705.6 85.7 %all-reduce.33.cloned.1.call-done = f32[1,784,640]{1,0,2:T(1,128)} async-done(((f32[1,784,640]{1,0,2:T(1,128)}), f32[1,784,640]{1,0,2:T(1,128)}) %all-reduce.33.cloned.1.call-update) | async-done | bytes 2007056
  793.1 30.5 %all_gather.22 = bf16[1,784,640]{1,2,0:T(8,128)(2,1)S(1)} all-gather(bf16[1,784,80]{1,2,0:T(8,128)(2,1)S(1)} %fusion.85), channel_id=1, replica_groups=mesh['section'=2,'cin'=8,'cout'=8] {'cout'}, dimensions={2}, use_global_device_ids=true | all-gather | bytes 1128960 | tf_op jit(solution)/shard_map/all_gather | solution.py:137
  829.1 3.6 reshape.211
  834.4 5.0 fusion.137
  842.4 2.5 fusion.19
  844.8 2.4 fusion.18
  848.8 45.4 %reduce-scatter.16.cloned.1.call-done = f32[1,784,40]{1,2,0:T(8,128)} async-done(((f32[1,784,320]{1,2,0:T(8,128)}), f32[1,784,40]{1,2,0:T(8,128)}) %reduce-scatter.16.cloned.1.call-update) | async-done | bytes 125456
  895.2 35.5 %all_gather.23 = bf16[1,784,320]{1,2,0:T(8,128)(2,1)S(1)} all-gather(bf16[1,784,40]{1,2,0:T(8,128)(2,1)S(1)} %multiply_convert_fusion.3), channel_id=1, replica_groups=mesh['section'=2,'cin'=8,'cout'=8] {'cin'}, dimensions={2}, use_global_device_ids=true | all-gather | bytes 564480 | tf_op jit(solution)/shard_map/all_gather | solution.py:141
  931.0 2.3 fusion.21
  933.5 2.4 fusion.23
  935.9 2.4 fusion.25
  945.8 2.7 pad_slice_fusion.4
  948.7 2.4 reshape.202
  955.4 2.6 fusion.95
  989.5 3.0 all-reduce.35.cloned.1.call-done
  994.5 4.1 convert_element_type.43
  998.5 37.7 %reduce-scatter.18.cloned.1.call-done = f32[1,784,40]{1,2,0:T(8,128)} async-done(((f32[1,784,320]{1,2,0:T(8,128)}), f32[1,784,40]{1,2,0:T(8,128)}) %reduce-scatter.18.cloned.1.call-update) | async-done | bytes 125456
  (223 shorter events, 110.4 us)
Async XLA Ops:
  8.0 459.5 %copy-start = (bf16[320,640]{1,0:T(8,128)(2,1)S(1)}, bf16[320,640]{1,0:T(8,128)(2,1)}, u32[]{:S(2)}) copy-start(bf16[320,640]{1,0:T(8,128)(2,1)} %param.11) | copy-start | bytes 1228804
  8.0 270.3 %reduce-scatter.14.cloned.1.call-start = ((), (), s32[]{:S(2)}) async-start(), calls=%async_computation.10 | async-start | bytes 1290240
  53.5 6.6 copy-start.1
  60.0 1.7 copy-start.27
  60.0 2.3 copy-start.26
  68.2 1.6 copy-start.49
  69.8 253.2 %all-reduce.25.cloned.1.call-start = ((), (), s32[]{:S(2)}) async-start(), calls=%async_computation.5 | async-start | bytes 8028160 | tf_op jit(solution)/shard_map/psum | solution.py:175
  99.4 4.2 copy-start.11
  245.2 18.2 %slice-start = ((s8[4587520]{0:T(1024)(128)(4,1)}), s8[393216]{0:T(1024)(128)(4,1)S(1)}, s32[]{:S(2)}) async-start(s8[4587520]{0:T(1024)(128)(4,1)} %bitcast.323), calls=%async_computation.14 | async-start | bytes 786432
  256.4 7.0 slice-start.1
  278.3 128.2 %all-reduce.31.cloned.1.call-start = ((), (), s32[]{:S(2)}) async-start(), calls=%async_computation.8 | async-start | bytes 4587520
  322.8 197.9 %all-reduce.27.cloned.1.call-start = ((), (), s32[]{:S(2)}) async-start(), calls=%async_computation.6 | async-start | bytes 8028160 | tf_op jit(solution)/shard_map/psum | solution.py:175
  322.9 84.6 %copy-start.47 = (bf16[1,784,80]{1,2,0:T(8,128)(2,1)S(1)}, bf16[1,784,80]{1,2,0:T(8,128)(2,1)}, u32[]{:S(2)}) copy-start(bf16[1,784,80]{1,2,0:T(8,128)(2,1)} %param.8) | copy-start | bytes 376324
  323.4 366.3 %all-reduce.29.cloned.1.call-start = ((), (), s32[]{:S(2)}) async-start(), calls=%async_computation.7 | async-start | bytes 8028160 | tf_op jit(solution)/shard_map/psum | solution.py:173
  470.9 320.3 %all-reduce.33.cloned.1.call-start = ((), (), s32[]{:S(2)}) async-start(), calls=%async_computation.9 | async-start | bytes 4587520
  694.8 1.3 copy-start.3
  705.5 86.8 %copy-start.15 = (f32[1,784,80]{1,0,2:T(1,128)S(1)}, f32[1,784,80]{1,0,2:T(1,128)}, u32[]{:S(2)}) copy-start(f32[1,784,80]{1,0,2:T(1,128)} %copy-done.14) | copy-start | bytes 752644
  705.5 119.2 %copy-start.44 = (bf16[320,640]{1,0:T(8,128)(2,1)S(1)}, bf16[320,640]{1,0:T(8,128)(2,1)}, u32[]{:S(2)}) copy-start(bf16[320,640]{1,0:T(8,128)(2,1)} %param.10) | copy-start | bytes 1228804
  705.5 188.7 %reduce-scatter.16.cloned.1.call-start = ((), (), s32[]{:S(2)}) async-start(), calls=%async_computation.11 | async-start | bytes 1290240
  824.7 1.9 copy-start.13
  826.4 166.2 %all-reduce.35.cloned.1.call-start = ((), (), s32[]{:S(2)}) async-start(), calls=%async_computation.13 | async-start | bytes 5242880 | tf_op jit(solution)/shard_map/psum | solution.py:191
  829.1 3.7 copy-start.5
  841.4 5.9 copy-start.9
  842.4 4.9 copy-start.34
  844.8 49.3 %copy-start.48 = (f32[1,784,40]{1,2,0:T(8,128)S(1)}, f32[1,784,40]{1,2,0:T(8,128)}, u32[]{:S(2)}) copy-start(f32[1,784,40]{1,2,0:T(8,128)} %reduce-scatter.14.cloned.1.call-done) | copy-start | bytes 376324
  930.6 13.9 %copy-start.6 = (bf16[1,784,320]{1,2,0:T(8,128)(2,1)}, bf16[1,784,320]{1,2,0:T(8,128)(2,1)S(1)}, u32[]{:S(2)}) copy-start(bf16[1,784,320]{1,2,0:T(8,128)(2,1)S(1)} %all_gather.23) | copy-start | bytes 1505284
  933.5 4.8 copy-start.25
  935.9 4.9 copy-start.23
  938.3 3.7 copy-start.21
  939.5 3.7 copy-start.19
  940.7 3.8 copy-start.17
  948.7 6.7 copy-start.2
  966.6 69.6 %reduce-scatter.18.cloned.1.call-start = ((), (), s32[]{:S(2)}) async-start(), calls=%async_computation.12 | async-start | bytes 1290240
  966.9 1.7 copy-start.30
  966.9 2.2 copy-start.31
  969.2 1.1 copy-start.29
  969.7 1.1 copy-start.28
  971.4 1.4 copy-start.10
  972.8 1.6 copy-start.41
  974.4 1.4 copy-start.40
  974.4 1.6 copy-start.39
  975.8 1.3 copy-start.38
  976.1 2.0 copy-start.37
  977.1 1.2 copy-start.36
  979.4 4.1 copy-start.43
  980.7 4.1 copy-start.42
  983.5 4.1 copy-start.4
  983.5 4.1 copy-start.45
  (14 other events, 13.3 us)
Sparse Core Ops, SparseCore 0:
  69.9 69.3 reduce-scatter.13
  826.5 67.6 reduce-scatter.15
Sparse Core Ops, SparseCore 1:
  278.4 34.6 all-reduce.24
  322.9 83.5 all-reduce.30
  409.1 111.6 all-reduce.26
  523.9 165.7 all-reduce.28
  705.6 85.6 all-reduce.32
  966.7 25.8 all-reduce.34
  995.4 40.8 reduce-scatter.17
